TPU v7x, 32 devices: a whole 2x2x4 slice. The times are simulated.
32 devices in a mesh: lat: 8 (over z, core), lon: 4 (over y, x).
Axes of the slice: x: 2, y: 2, z: 4, core: 2. Of those that a mesh axis runs over, the one named last changes fastest.
Arguments:
- misfit: float32 [8, 256, 512], P(None, 'lat', 'lon'), may hold values from -6 to 6
- flow_east: float32 [8, 256, 512], P(None, 'lat', 'lon'), may hold values from -6 to 6
- flow_north: float32 [8, 256, 512], P(None, 'lat', 'lon'), may hold values from -6 to 6
- ocean_depth: float32 [256, 512], P('lat', 'lon'), may hold values from 0.4 to 1.6
- drag_rate: float32 [256, 512], P('lat', 'lon'), may hold values from 0.02 to 0.3
- wet_mask: int32 [256, 512], P('lat', 'lon'), may hold values from 0 to 1, as said below
- legendre: bfloat16 [256, 256, 1024], P(('lon', 'lat')), as said below
- love_factor: float32 [256], replicated, may hold values from 0.2 to 2
- assignment: int32 [256], replicated, may hold values from 0 to 255, as said below
Outputs:
- adjoint_height: float32 [8, 256, 512], P(None, 'lat', 'lon')
- adjoint_east: float32 [8, 256, 512], P(None, 'lat', 'lon')
- adjoint_north: float32 [8, 256, 512], P(None, 'lat', 'lon')
Inputs may be any that keep to these rules, and one draw needn't show every extreme that they name: `wet_mask`: 1 marks a wet cell and 0 land; the first and the last latitude rows are land. `assignment`: A permutation: each of the 256 orders appears once. `legendre`: entry [p, a, n] belongs to degree assignment[p] + n and is zero where assignment[p] + n >= 256.
All inputs are finite; a program needn't handle non-finite values.
Results may differ from a plain program's by a relative error of at most 0.0028.
Values may be sent and summed in bfloat16 or wider, within the bound.
A program may use at most 64 MiB of HBM per device.

v0:
```python
import math
import jax
import jax.numpy as jnp
from jax import lax
from jax.sharding import PartitionSpec as P

TIME_STEPS = 4
TWO_PI = 2.0 * math.pi
exact_mode = lax.Precision.HIGHEST


def with_halo(cells, sides, width):
    for axis, dim in sides:
        count = lax.axis_size(axis)
        head = lax.slice_in_dim(cells, 0, width, axis=dim)
        tail = lax.slice_in_dim(cells, cells.shape[dim] - width, cells.shape[dim], axis=dim)
        cells = jnp.concatenate(
            [
                lax.ppermute(tail, axis, [(i, (i + 1) % count) for i in range(count)]),
                cells,
                lax.ppermute(head, axis, [((i + 1) % count, i) for i in range(count)]),
            ],
            axis=dim,
        )
    return cells


def extend(stacked):
    return with_halo(stacked, (("lat", 2), ("lon", 3)), 1)


def differences(extended):
    east_diff = extended[:, :, 1:-1, 2:] - extended[:, :, 1:-1, :-2]
    north_diff = extended[:, :, 2:, 1:-1] - extended[:, :, :-2, 1:-1]
    return (east_diff, north_diff)


def adjoint_step(height, east_flow, north_flow, wetness, ocean_depth, drag_rate):
    east_diff, north_diff = differences(extend(height[None]))
    retained = 1.0 - drag_rate
    east_flow = wetness * (retained * east_flow - 0.5 * east_diff[0])
    north_flow = wetness * (retained * north_flow - 0.5 * north_diff[0])
    flow_east_diff, flow_north_diff = differences(extend(jnp.stack([east_flow, north_flow])))
    height = wetness * (height - 0.5 * ocean_depth * (flow_east_diff[0] + flow_north_diff[1]))
    return (height, east_flow, north_flow)


def phases(orders, positions, period):
    products = orders[:, None] * positions[None, :] % period
    radians = products.astype(jnp.float32) * (TWO_PI / period)
    return (jnp.cos(radians), jnp.sin(radians))


def spherical(spectra, legendre, weights, lat_count, row_count):
    slot_count = legendre.shape[0]
    degree_count = legendre.shape[2]
    legendre_blocks = legendre.reshape(slot_count, lat_count, row_count, degree_count)
    spectra_blocks = spectra.reshape(slot_count, lat_count, -1, row_count)
    coefficients = jnp.einsum(
        "kicr,kirn->kcn", spectra_blocks, legendre_blocks, preferred_element_type=jnp.float32
    )
    coefficients = (coefficients * weights[:, None, :]).astype(jnp.bfloat16)
    synthesis = jnp.einsum(
        "kcn,kirn->kicr", coefficients, legendre_blocks, preferred_element_type=jnp.float32
    )
    return synthesis.astype(jnp.bfloat16)


def local(
    misfit,
    flow_east,
    flow_north,
    ocean_depth,
    drag_rate,
    wet_mask,
    legendre,
    love_factor,
    assignment,
):
    field_count, row_count, col_count = misfit.shape
    lat_count = lax.axis_size("lat")
    lon_count = lax.axis_size("lon")
    period = col_count * lon_count
    order_count = period // 2
    slot_count = legendre.shape[0]
    degree_count = legendre.shape[2]
    row_pair = row_count // lon_count
    lat_index = lax.axis_index("lat")
    lon_index = lax.axis_index("lon")
    wetness = wet_mask.astype(jnp.float32)
    height = wetness * misfit
    east_flow = wetness * flow_east
    north_flow = wetness * flow_north

    def advance(height, east_flow, north_flow):
        return adjoint_step(height, east_flow, north_flow, wetness, ocean_depth, drag_rate)

    for _ in range(TIME_STEPS):
        height, east_flow, north_flow = advance(height, east_flow, north_flow)
    base = (lon_index * lat_count + lat_index) * slot_count
    my_orders = lax.dynamic_slice_in_dim(assignment, base, slot_count)
    love_pad = jnp.concatenate([love_factor, jnp.zeros((degree_count,), jnp.float32)])
    weights = jax.vmap(
        lambda first_order: lax.dynamic_slice_in_dim(love_pad, first_order, degree_count)
    )(my_orders)
    all_cells = jnp.arange(period, dtype=jnp.int32)
    cos_full, sin_full = phases(assignment, all_cells, period)
    row_block = lax.all_to_all(height, "lon", split_axis=1, concat_axis=2, tiled=True)
    real_part = jnp.einsum("nrx,mx->nrm", row_block, cos_full, precision=exact_mode)
    imag_part = -jnp.einsum("nrx,mx->nrm", row_block, sin_full, precision=exact_mode)
    rowwise = jnp.stack([real_part, imag_part], 2).astype(jnp.bfloat16)
    gathered = rowwise.transpose(3, 2, 0, 1).reshape(lon_count, lat_count, -1)
    received = lax.all_to_all(
        lax.all_to_all(gathered, "lat", split_axis=1, concat_axis=1, tiled=True),
        "lon",
        split_axis=0,
        concat_axis=0,
        tiled=True,
    )
    received = received.reshape(lon_count, lat_count, slot_count, 2, field_count, row_pair)
    spectra = received.transpose(2, 1, 3, 4, 0, 5).reshape(
        slot_count, lat_count, 2 * field_count * row_count
    )
    synthesis = spherical(spectra, legendre, weights, lat_count, row_count)
    arranged = synthesis.reshape(slot_count, lat_count, 2, field_count, lon_count, row_pair)
    arranged = arranged.transpose(4, 1, 0, 2, 3, 5).reshape(lon_count, lat_count, -1)
    returned = lax.all_to_all(
        lax.all_to_all(arranged, "lat", split_axis=1, concat_axis=1, tiled=True),
        "lon",
        split_axis=0,
        concat_axis=0,
        tiled=True,
    )
    returned = returned.reshape(order_count, 2, field_count, row_pair).astype(jnp.float32)
    doubling = jnp.where(assignment == 0, 1.0, 2.0).astype(jnp.float32)
    grid_rows = jnp.einsum(
        "mx,mfr->frx", cos_full * doubling[:, None], returned[:, 0], precision=exact_mode
    ) - jnp.einsum(
        "mx,mfr->frx", sin_full * doubling[:, None], returned[:, 1], precision=exact_mode
    )
    loading = lax.all_to_all(grid_rows, "lon", split_axis=2, concat_axis=1, tiled=True)
    height = height + wetness * loading
    return advance(height, east_flow, north_flow)


def solution(mesh):
    placed = (
        P(None, "lat", "lon"),
        P(None, "lat", "lon"),
        P(None, "lat", "lon"),
        P("lat", "lon"),
        P("lat", "lon"),
        P("lat", "lon"),
        P(("lon", "lat"), None, None),
        P(),
        P(),
    )
    return jax.shard_map(
        local,
        mesh=mesh,
        in_specs=placed,
        out_specs=(P(None, "lat", "lon"), P(None, "lat", "lon"), P(None, "lat", "lon")),
        check_vma=False,
    )
```

profile of v0, /device:TPU:0, one launch (start us, length us, event | category | flops | bytes accessed | tf_op | source)
XLA Modules:
  0.0 253.9 jit_solution(16418631101517796318)
XLA Ops:
  2.9 4.1 %collective-permute-start.1 = (f32[1,8,1,128]{3,1,2,0:T(8,128)S(1)}, f32[1,8,1,128]{3,1,2,0:T(8,128)S(1)}, u32[]{:S(2)}, u32[]{:S(2)}) collective-permute-start(f32[1,8,1,128]{3,1,2,0:T(8,128)S(1)} %get-tuple-element.71), channel_id=1, source_target_pairs={{4,0},{8,4},{12,8},{16,12},{20,16},{24,20},{28,24},{0,28},{5,1},{9... | collective-permute-start | bytes 12296 | tf_op jit(solution)/shard_map/ppermute | solution.py:21
  12.1 3.3 %collective-permute-done.2 = f32[1,8,34,1]{3,1,2,0:T(8,128)S(1)} collective-permute-done((f32[1,8,34,1]{3,1,2,0:T(8,128)S(1)}, f32[1,8,34,1]{3,1,2,0:T(8,128)S(1)}, u32[]{:S(2)}, u32[]{:S(2)}) %collective-permute-start.2) | collective-permute-done | bytes 1120 | tf_op jit(solution)/shard_map/ppermute | solution.py:21
  19.8 3.5 %collective-permute-start.5 = (f32[2,8,1,128]{3,1,2,0:T(8,128)S(1)}, f32[2,8,1,128]{3,1,2,0:T(8,128)S(1)}, u32[]{:S(2)}, u32[]{:S(2)}) collective-permute-start(f32[2,8,1,128]{3,1,2,0:T(8,128)S(1)} %get-tuple-element.46), channel_id=1, source_target_pairs={{4,0},{8,4},{12,8},{16,12},{20,16},{24,20},{28,24},{0,28},{5,1},{9... | collective-permute-start | bytes 24584 | tf_op jit(solution)/shard_map/ppermute | solution.py:21
  27.7 6.8 %collective-permute-done.6 = f32[2,8,34,1]{3,1,2,0:T(8,128)S(1)} collective-permute-done((f32[2,8,34,1]{3,1,2,0:T(8,128)S(1)}, f32[2,8,34,1]{3,1,2,0:T(8,128)S(1)}, u32[]{:S(2)}, u32[]{:S(2)}) %collective-permute-start.6) | collective-permute-done | bytes 2208 | tf_op jit(solution)/shard_map/ppermute | solution.py:21
  34.5 3.3 %collective-permute-done.7 = f32[2,8,34,1]{3,1,2,0:T(8,128)S(1)} collective-permute-done((f32[2,8,34,1]{3,1,2,0:T(8,128)S(1)}, f32[2,8,34,1]{3,1,2,0:T(8,128)S(1)}, u32[]{:S(2)}, u32[]{:S(2)}) %collective-permute-start.7) | collective-permute-done | bytes 2208 | tf_op jit(solution)/shard_map/ppermute | solution.py:19
  38.0 3.5 %collective-permute-start.9 = (f32[1,8,1,128]{3,1,2,0:T(8,128)S(1)}, f32[1,8,1,128]{3,1,2,0:T(8,128)S(1)}, u32[]{:S(2)}, u32[]{:S(2)}) collective-permute-start(f32[1,8,1,128]{3,1,2,0:T(8,128)S(1)} %get-tuple-element.69), channel_id=1, source_target_pairs={{4,0},{8,4},{12,8},{16,12},{20,16},{24,20},{28,24},{0,28},{5,1},{9... | collective-permute-start | bytes 12296 | tf_op jit(solution)/shard_map/ppermute | solution.py:21
  45.4 3.7 %collective-permute-done.10 = f32[1,8,34,1]{3,1,2,0:T(8,128)S(1)} collective-permute-done((f32[1,8,34,1]{3,1,2,0:T(8,128)S(1)}, f32[1,8,34,1]{3,1,2,0:T(8,128)S(1)}, u32[]{:S(2)}, u32[]{:S(2)}) %collective-permute-start.10) | collective-permute-done | bytes 1120 | tf_op jit(solution)/shard_map/ppermute | solution.py:21
  51.8 3.5 %collective-permute-start.13 = (f32[2,8,1,128]{3,1,2,0:T(8,128)S(1)}, f32[2,8,1,128]{3,1,2,0:T(8,128)S(1)}, u32[]{:S(2)}, u32[]{:S(2)}) collective-permute-start(f32[2,8,1,128]{3,1,2,0:T(8,128)S(1)} %get-tuple-element.44), channel_id=1, source_target_pairs={{4,0},{8,4},{12,8},{16,12},{20,16},{24,20},{28,24},{0,28},{5,1},{9... | collective-permute-start | bytes 24584 | tf_op jit(solution)/shard_map/ppermute | solution.py:21
  59.0 7.5 %collective-permute-done.14 = f32[2,8,34,1]{3,1,2,0:T(8,128)S(1)} collective-permute-done((f32[2,8,34,1]{3,1,2,0:T(8,128)S(1)}, f32[2,8,34,1]{3,1,2,0:T(8,128)S(1)}, u32[]{:S(2)}, u32[]{:S(2)}) %collective-permute-start.14) | collective-permute-done | bytes 2208 | tf_op jit(solution)/shard_map/ppermute | solution.py:21
  69.6 3.5 %collective-permute-start.17 = (f32[1,8,1,128]{3,1,2,0:T(8,128)S(1)}, f32[1,8,1,128]{3,1,2,0:T(8,128)S(1)}, u32[]{:S(2)}, u32[]{:S(2)}) collective-permute-start(f32[1,8,1,128]{3,1,2,0:T(8,128)S(1)} %get-tuple-element.67), channel_id=1, source_target_pairs={{4,0},{8,4},{12,8},{16,12},{20,16},{24,20},{28,24},{0,28},{5,1},{9... | collective-permute-start | bytes 12296 | tf_op jit(solution)/shard_map/ppermute | solution.py:21
  76.7 3.2 %collective-permute-done.18 = f32[1,8,34,1]{3,1,2,0:T(8,128)S(1)} collective-permute-done((f32[1,8,34,1]{3,1,2,0:T(8,128)S(1)}, f32[1,8,34,1]{3,1,2,0:T(8,128)S(1)}, u32[]{:S(2)}, u32[]{:S(2)}) %collective-permute-start.18) | collective-permute-done | bytes 1120 | tf_op jit(solution)/shard_map/ppermute | solution.py:21
  82.8 3.5 %collective-permute-start.21 = (f32[2,8,1,128]{3,1,2,0:T(8,128)S(1)}, f32[2,8,1,128]{3,1,2,0:T(8,128)S(1)}, u32[]{:S(2)}, u32[]{:S(2)}) collective-permute-start(f32[2,8,1,128]{3,1,2,0:T(8,128)S(1)} %get-tuple-element.42), channel_id=1, source_target_pairs={{4,0},{8,4},{12,8},{16,12},{20,16},{24,20},{28,24},{0,28},{5,1},{9... | collective-permute-start | bytes 24584 | tf_op jit(solution)/shard_map/ppermute | solution.py:21
  89.9 7.4 %collective-permute-done.22 = f32[2,8,34,1]{3,1,2,0:T(8,128)S(1)} collective-permute-done((f32[2,8,34,1]{3,1,2,0:T(8,128)S(1)}, f32[2,8,34,1]{3,1,2,0:T(8,128)S(1)}, u32[]{:S(2)}, u32[]{:S(2)}) %collective-permute-start.22) | collective-permute-done | bytes 2208 | tf_op jit(solution)/shard_map/ppermute | solution.py:21
  100.5 3.5 %collective-permute-start.25 = (f32[1,8,1,128]{3,1,2,0:T(8,128)S(1)}, f32[1,8,1,128]{3,1,2,0:T(8,128)S(1)}, u32[]{:S(2)}, u32[]{:S(2)}) collective-permute-start(f32[1,8,1,128]{3,1,2,0:T(8,128)S(1)} %get-tuple-element.65), channel_id=1, source_target_pairs={{4,0},{8,4},{12,8},{16,12},{20,16},{24,20},{28,24},{0,28},{5,1},{9... | collective-permute-start | bytes 12296 | tf_op jit(solution)/shard_map/ppermute | solution.py:21
  113.3 3.5 %collective-permute-start.29 = (f32[2,8,1,128]{3,1,2,0:T(8,128)S(1)}, f32[2,8,1,128]{3,1,2,0:T(8,128)S(1)}, u32[]{:S(2)}, u32[]{:S(2)}) collective-permute-start(f32[2,8,1,128]{3,1,2,0:T(8,128)S(1)} %get-tuple-element.40), channel_id=1, source_target_pairs={{4,0},{8,4},{12,8},{16,12},{20,16},{24,20},{28,24},{0,28},{5,1},{9... | collective-permute-start | bytes 24584 | tf_op jit(solution)/shard_map/ppermute | solution.py:21
  120.4 7.5 %collective-permute-done.30 = f32[2,8,34,1]{3,1,2,0:T(8,128)S(1)} collective-permute-done((f32[2,8,34,1]{3,1,2,0:T(8,128)S(1)}, f32[2,8,34,1]{3,1,2,0:T(8,128)S(1)}, u32[]{:S(2)}, u32[]{:S(2)}) %collective-permute-start.30) | collective-permute-done | bytes 2208 | tf_op jit(solution)/shard_map/ppermute | solution.py:21
  127.9 3.2 %collective-permute-done.31 = f32[2,8,34,1]{3,1,2,0:T(8,128)S(1)} collective-permute-done((f32[2,8,34,1]{3,1,2,0:T(8,128)S(1)}, f32[2,8,34,1]{3,1,2,0:T(8,128)S(1)}, u32[]{:S(2)}, u32[]{:S(2)}) %collective-permute-start.31) | collective-permute-done | bytes 2208 | tf_op jit(solution)/shard_map/ppermute | solution.py:19
  131.3 7.7 %all_to_all.56 = f32[8,32,128]{2,0,1:T(8,128)S(1)} all-to-all(f32[8,32,128]{2,0,1:T(8,128)S(1)} %fusion.51), channel_id=1, replica_groups=mesh['lat'=8,'lon'=4] {'lon'}, dimensions={1} | all-to-all | bytes 262144 | tf_op jit(solution)/shard_map/all_to_all | solution.py:108
  147.2 3.4 %all-to-all-start.1 = ((bf16[4,8,1024]{2,0,1:T(4,128)(2,1)}), bf16[4,8,1024]{2,0,1:T(4,128)(2,1)S(1)}, u32[]{:S(2)}, u32[]{:S(2)}) async-start(bf16[4,8,1024]{2,0,1:T(4,128)(2,1)} %copy.39), calls=%async_computation.1 | async-start | bytes 131072 | tf_op jit(solution)/shard_map/all_to_all | solution.py:114
  150.6 5.8 %all-to-all-done.1 = bf16[4,8,1024]{2,0,1:T(4,128)(2,1)S(1)} async-done(((bf16[4,8,1024]{2,0,1:T(4,128)(2,1)}), bf16[4,8,1024]{2,0,1:T(4,128)(2,1)S(1)}, u32[]{:S(2)}, u32[]{:S(2)}) %all-to-all-start.1) | async-done | bytes 65568 | tf_op jit(solution)/shard_map/all_to_all | solution.py:114
  157.1 3.5 %all-to-all-start.2 = ((bf16[4,8,1024]{2,1,0:T(8,128)(2,1)}), bf16[4,8,1024]{2,1,0:T(8,128)(2,1)S(1)}, u32[]{:S(2)}, u32[]{:S(2)}) async-start(bf16[4,8,1024]{2,1,0:T(8,128)(2,1)} %copy.40), calls=%async_computation.2 | async-start | bytes 131072 | tf_op jit(solution)/shard_map/all_to_all | solution.py:113
  160.7 11.2 %while.1 = (s32[]{:T(128)}, f32[1280]{0:T(1024)S(1)}, s32[8,1]{0,1:T(1,128)S(1)}, f32[8,1024]{1,0:T(8,128)S(1)}, s32[]{:T(128)}, /*index=5*/s32[]{:T(128)}) while((s32[]{:T(128)}, f32[1280]{0:T(1024)S(1)}, s32[8,1]{0,1:T(1,128)S(1)}, f32[8,1024]{1,0:T(8,128)S(1)}, s32[]{:T(128)}, /*index=5*/s32[]{:T(128)}) %tuple.46), condition=%wide.while_cond, body=%wide.while_body.sunk | while | flops 2 | bytes 16473 | solution.py:104
  175.0 7.1 %fusion.3 = bf16[8,8,16,32]{3,2,1,0:T(8,128)(2,1)S(1)} fusion(bf16[8,8,32,1024]{3,2,1,0:T(8,128)(2,1)} %bitcast.210, bf16[8,8,16,32]{3,2,1,0:T(8,128)(2,1)S(1)} %reshape_reshape.3, f32[8,1024]{1,0:T(8,128)S(1)} %get-tuple-element.10), kind=kOutput, calls=%fused_computation.6 | convolution fusion | flops 134512640 | bytes 4358144 | tf_op jit(solution)/shard_map/kcn,kirn->kicr/dot_general | solution.py:63
  184.2 8.3 %all_to_all.57 = bf16[4,8,1024]{2,0,1:T(4,128)(2,1)S(1)} all-to-all(bf16[4,8,1024]{2,0,1:T(4,128)(2,1)S(1)} %copy.43), channel_id=1, replica_groups=mesh['lat'=8,'lon'=4] {'lat'}, dimensions={1} | all-to-all | bytes 131072 | tf_op jit(solution)/shard_map/all_to_all | solution.py:128
  193.2 3.9 %all-to-all-start.4 = ((bf16[4,8,1024]{2,1,0:T(8,128)(2,1)}), bf16[4,8,1024]{2,1,0:T(8,128)(2,1)S(1)}, u32[]{:S(2)}, u32[]{:S(2)}) async-start(bf16[4,8,1024]{2,1,0:T(8,128)(2,1)} %copy.44), calls=%async_computation.4 | async-start | bytes 131072 | tf_op jit(solution)/shard_map/all_to_all | solution.py:127
  197.1 4.8 %all-to-all-done.4 = bf16[4,8,1024]{2,1,0:T(8,128)(2,1)S(1)} async-done(((bf16[4,8,1024]{2,1,0:T(8,128)(2,1)}), bf16[4,8,1024]{2,1,0:T(8,128)(2,1)S(1)}, u32[]{:S(2)}, u32[]{:S(2)}) %all-to-all-start.4) | async-done | bytes 65568 | tf_op jit(solution)/shard_map/all_to_all | solution.py:127
  210.3 7.4 %all_to_all.58 = f32[4,1,8192]{2,1,0:T(1,128)S(1)} all-to-all(f32[4,1,8192]{2,1,0:T(1,128)S(1)} %reshape.81), channel_id=1, replica_groups=mesh['lat'=8,'lon'=4] {'lon'}, dimensions={0} | all-to-all | bytes 262144 | tf_op jit(solution)/shard_map/all_to_all | solution.py:141
  221.1 3.5 %collective-permute-start.33 = (f32[1,8,1,128]{3,1,2,0:T(8,128)S(1)}, f32[1,8,1,128]{3,1,2,0:T(8,128)S(1)}, u32[]{:S(2)}, u32[]{:S(2)}) collective-permute-start(f32[1,8,1,128]{3,1,2,0:T(8,128)S(1)} %get-tuple-element.63), channel_id=1, source_target_pairs={{4,0},{8,4},{12,8},{16,12},{20,16},{24,20},{28,24},{0,28},{5,1},{9... | collective-permute-start | bytes 12296 | tf_op jit(solution)/shard_map/ppermute | solution.py:21
  228.2 4.3 %collective-permute-done.34 = f32[1,8,34,1]{3,1,2,0:T(8,128)S(1)} collective-permute-done((f32[1,8,34,1]{3,1,2,0:T(8,128)S(1)}, f32[1,8,34,1]{3,1,2,0:T(8,128)S(1)}, u32[]{:S(2)}, u32[]{:S(2)}) %collective-permute-start.34) | collective-permute-done | bytes 1120 | tf_op jit(solution)/shard_map/ppermute | solution.py:21
  234.6 3.5 %collective-permute-start.37 = (f32[2,8,1,128]{3,1,2,0:T(8,128)S(1)}, f32[2,8,1,128]{3,1,2,0:T(8,128)S(1)}, u32[]{:S(2)}, u32[]{:S(2)}) collective-permute-start(f32[2,8,1,128]{3,1,2,0:T(8,128)S(1)} %get-tuple-element.38), channel_id=1, source_target_pairs={{4,0},{8,4},{12,8},{16,12},{20,16},{24,20},{28,24},{0,28},{5,1},{9... | collective-permute-start | bytes 24584 | tf_op jit(solution)/shard_map/ppermute | solution.py:21
  243.1 6.1 %collective-permute-done.38 = f32[2,8,34,1]{3,1,2,0:T(8,128)S(1)} collective-permute-done((f32[2,8,34,1]{3,1,2,0:T(8,128)S(1)}, f32[2,8,34,1]{3,1,2,0:T(8,128)S(1)}, u32[]{:S(2)}, u32[]{:S(2)}) %collective-permute-start.38) | collective-permute-done | bytes 2208 | tf_op jit(solution)/shard_map/ppermute | solution.py:21
  249.2 3.8 %collective-permute-done.39 = f32[2,8,34,1]{3,1,2,0:T(8,128)S(1)} collective-permute-done((f32[2,8,34,1]{3,1,2,0:T(8,128)S(1)}, f32[2,8,34,1]{3,1,2,0:T(8,128)S(1)}, u32[]{:S(2)}, u32[]{:S(2)}) %collective-permute-start.39) | collective-permute-done | bytes 2208 | tf_op jit(solution)/shard_map/ppermute | solution.py:19
  (170 shorter events, 104.5 us)
Async XLA Ops:
  2.4 5.9 %collective-permute-start = (f32[1,8,1,128]{3,1,2,0:T(8,128)S(1)}, f32[1,8,1,128]{3,1,2,0:T(8,128)S(1)}, u32[]{:S(2)}, u32[]{:S(2)}) collective-permute-start(f32[1,8,1,128]{3,1,2,0:T(8,128)S(1)} %get-tuple-element.72), channel_id=1, source_target_pairs={{0,4},{4,8},{8,12},{12,16},{16,20},{20,24},{24,28},{28,0},{1,5},{5... | collective-permute-start | bytes 12296 | tf_op jit(solution)/shard_map/ppermute | solution.py:19
  2.9 5.4 %collective-permute-start.1 = (f32[1,8,1,128]{3,1,2,0:T(8,128)S(1)}, f32[1,8,1,128]{3,1,2,0:T(8,128)S(1)}, u32[]{:S(2)}, u32[]{:S(2)}) collective-permute-start(f32[1,8,1,128]{3,1,2,0:T(8,128)S(1)} %get-tuple-element.71), channel_id=1, source_target_pairs={{4,0},{8,4},{12,8},{16,12},{20,16},{24,20},{28,24},{0,28},{5,1},{9... | collective-permute-start | bytes 12296 | tf_op jit(solution)/shard_map/ppermute | solution.py:21
  8.5 7.0 %collective-permute-start.2 = (f32[1,8,34,1]{3,1,2,0:T(8,128)S(1)}, f32[1,8,34,1]{3,1,2,0:T(8,128)S(1)}, u32[]{:S(2)}, u32[]{:S(2)}) collective-permute-start(f32[1,8,34,1]{3,1,2,0:T(8,128)S(1)} %get-tuple-element.61), channel_id=1, source_target_pairs={{1,0},{2,1},{3,2},{0,3},{5,4},{6,5},{7,6},{4,7},{9,8},{10,9},{11,1... | collective-permute-start | bytes 3272 | tf_op jit(solution)/shard_map/ppermute | solution.py:21
  11.4 7.1 %collective-permute-start.3 = (f32[1,8,34,1]{3,1,2,0:T(8,128)S(1)}, f32[1,8,34,1]{3,1,2,0:T(8,128)S(1)}, u32[]{:S(2)}, u32[]{:S(2)}) collective-permute-start(f32[1,8,34,1]{3,1,2,0:T(8,128)S(1)} %get-tuple-element.62), channel_id=1, source_target_pairs={{0,1},{1,2},{2,3},{3,0},{4,5},{5,6},{6,7},{7,4},{8,9},{9,10},{10,1... | collective-permute-start | bytes 3272 | tf_op jit(solution)/shard_map/ppermute | solution.py:19
  19.8 4.9 %collective-permute-start.4 = (f32[2,8,1,128]{3,1,2,0:T(8,128)S(1)}, f32[2,8,1,128]{3,1,2,0:T(8,128)S(1)}, u32[]{:S(2)}, u32[]{:S(2)}) collective-permute-start(f32[2,8,1,128]{3,1,2,0:T(8,128)S(1)} %get-tuple-element.45), channel_id=1, source_target_pairs={{0,4},{4,8},{8,12},{12,16},{16,20},{20,24},{24,28},{28,0},{1,5},{5... | collective-permute-start | bytes 24584 | tf_op jit(solution)/shard_map/ppermute | solution.py:19
  19.8 4.9 %collective-permute-start.5 = (f32[2,8,1,128]{3,1,2,0:T(8,128)S(1)}, f32[2,8,1,128]{3,1,2,0:T(8,128)S(1)}, u32[]{:S(2)}, u32[]{:S(2)}) collective-permute-start(f32[2,8,1,128]{3,1,2,0:T(8,128)S(1)} %get-tuple-element.46), channel_id=1, source_target_pairs={{4,0},{8,4},{12,8},{16,12},{20,16},{24,20},{28,24},{0,28},{5,1},{9... | collective-permute-start | bytes 24584 | tf_op jit(solution)/shard_map/ppermute | solution.py:21
  24.9 9.6 %collective-permute-start.6 = (f32[2,8,34,1]{3,1,2,0:T(8,128)S(1)}, f32[2,8,34,1]{3,1,2,0:T(8,128)S(1)}, u32[]{:S(2)}, u32[]{:S(2)}) collective-permute-start(f32[2,8,34,1]{3,1,2,0:T(8,128)S(1)} %get-tuple-element.36), channel_id=1, source_target_pairs={{1,0},{2,1},{3,2},{0,3},{5,4},{6,5},{7,6},{4,7},{9,8},{10,9},{11,1... | collective-permute-start | bytes 6536 | tf_op jit(solution)/shard_map/ppermute | solution.py:21
  26.4 11.4 %collective-permute-start.7 = (f32[2,8,34,1]{3,1,2,0:T(8,128)S(1)}, f32[2,8,34,1]{3,1,2,0:T(8,128)S(1)}, u32[]{:S(2)}, u32[]{:S(2)}) collective-permute-start(f32[2,8,34,1]{3,1,2,0:T(8,128)S(1)} %get-tuple-element.35), channel_id=1, source_target_pairs={{0,1},{1,2},{2,3},{3,0},{4,5},{5,6},{6,7},{7,4},{8,9},{9,10},{10,1... | collective-permute-start | bytes 6536 | tf_op jit(solution)/shard_map/ppermute | solution.py:19
  43.0 6.1 %collective-permute-start.10 = (f32[1,8,34,1]{3,1,2,0:T(8,128)S(1)}, f32[1,8,34,1]{3,1,2,0:T(8,128)S(1)}, u32[]{:S(2)}, u32[]{:S(2)}) collective-permute-start(f32[1,8,34,1]{3,1,2,0:T(8,128)S(1)} %get-tuple-element.59), channel_id=1, source_target_pairs={{1,0},{2,1},{3,2},{0,3},{5,4},{6,5},{7,6},{4,7},{9,8},{10,9},{11,1... | collective-permute-start | bytes 3272 | tf_op jit(solution)/shard_map/ppermute | solution.py:21
  45.4 6.2 %collective-permute-start.11 = (f32[1,8,34,1]{3,1,2,0:T(8,128)S(1)}, f32[1,8,34,1]{3,1,2,0:T(8,128)S(1)}, u32[]{:S(2)}, u32[]{:S(2)}) collective-permute-start(f32[1,8,34,1]{3,1,2,0:T(8,128)S(1)} %get-tuple-element.60), channel_id=1, source_target_pairs={{0,1},{1,2},{2,3},{3,0},{4,5},{5,6},{6,7},{7,4},{8,9},{9,10},{10,1... | collective-permute-start | bytes 3272 | tf_op jit(solution)/shard_map/ppermute | solution.py:19
  51.8 4.9 %collective-permute-start.12 = (f32[2,8,1,128]{3,1,2,0:T(8,128)S(1)}, f32[2,8,1,128]{3,1,2,0:T(8,128)S(1)}, u32[]{:S(2)}, u32[]{:S(2)}) collective-permute-start(f32[2,8,1,128]{3,1,2,0:T(8,128)S(1)} %get-tuple-element.43), channel_id=1, source_target_pairs={{0,4},{4,8},{8,12},{12,16},{16,20},{20,24},{24,28},{28,0},{1,5},{5... | collective-permute-start | bytes 24584 | tf_op jit(solution)/shard_map/ppermute | solution.py:19
  56.9 9.6 %collective-permute-start.14 = (f32[2,8,34,1]{3,1,2,0:T(8,128)S(1)}, f32[2,8,34,1]{3,1,2,0:T(8,128)S(1)}, u32[]{:S(2)}, u32[]{:S(2)}) collective-permute-start(f32[2,8,34,1]{3,1,2,0:T(8,128)S(1)} %get-tuple-element.34), channel_id=1, source_target_pairs={{1,0},{2,1},{3,2},{0,3},{5,4},{6,5},{7,6},{4,7},{9,8},{10,9},{11,1... | collective-permute-start | bytes 6536 | tf_op jit(solution)/shard_map/ppermute | solution.py:21
  57.8 11.6 %collective-permute-start.15 = (f32[2,8,34,1]{3,1,2,0:T(8,128)S(1)}, f32[2,8,34,1]{3,1,2,0:T(8,128)S(1)}, u32[]{:S(2)}, u32[]{:S(2)}) collective-permute-start(f32[2,8,34,1]{3,1,2,0:T(8,128)S(1)} %get-tuple-element.33), channel_id=1, source_target_pairs={{0,1},{1,2},{2,3},{3,0},{4,5},{5,6},{6,7},{7,4},{8,9},{9,10},{10,1... | collective-permute-start | bytes 6536 | tf_op jit(solution)/shard_map/ppermute | solution.py:19
  74.6 5.3 %collective-permute-start.18 = (f32[1,8,34,1]{3,1,2,0:T(8,128)S(1)}, f32[1,8,34,1]{3,1,2,0:T(8,128)S(1)}, u32[]{:S(2)}, u32[]{:S(2)}) collective-permute-start(f32[1,8,34,1]{3,1,2,0:T(8,128)S(1)} %get-tuple-element.57), channel_id=1, source_target_pairs={{1,0},{2,1},{3,2},{0,3},{5,4},{6,5},{7,6},{4,7},{9,8},{10,9},{11,1... | collective-permute-start | bytes 3272 | tf_op jit(solution)/shard_map/ppermute | solution.py:21
  76.6 6.0 %collective-permute-start.19 = (f32[1,8,34,1]{3,1,2,0:T(8,128)S(1)}, f32[1,8,34,1]{3,1,2,0:T(8,128)S(1)}, u32[]{:S(2)}, u32[]{:S(2)}) collective-permute-start(f32[1,8,34,1]{3,1,2,0:T(8,128)S(1)} %get-tuple-element.58), channel_id=1, source_target_pairs={{0,1},{1,2},{2,3},{3,0},{4,5},{5,6},{6,7},{7,4},{8,9},{9,10},{10,1... | collective-permute-start | bytes 3272 | tf_op jit(solution)/shard_map/ppermute | solution.py:19
  82.7 4.9 %collective-permute-start.20 = (f32[2,8,1,128]{3,1,2,0:T(8,128)S(1)}, f32[2,8,1,128]{3,1,2,0:T(8,128)S(1)}, u32[]{:S(2)}, u32[]{:S(2)}) collective-permute-start(f32[2,8,1,128]{3,1,2,0:T(8,128)S(1)} %get-tuple-element.41), channel_id=1, source_target_pairs={{0,4},{4,8},{8,12},{12,16},{16,20},{20,24},{24,28},{28,0},{1,5},{5... | collective-permute-start | bytes 24584 | tf_op jit(solution)/shard_map/ppermute | solution.py:19
  82.8 4.9 %collective-permute-start.21 = (f32[2,8,1,128]{3,1,2,0:T(8,128)S(1)}, f32[2,8,1,128]{3,1,2,0:T(8,128)S(1)}, u32[]{:S(2)}, u32[]{:S(2)}) collective-permute-start(f32[2,8,1,128]{3,1,2,0:T(8,128)S(1)} %get-tuple-element.42), channel_id=1, source_target_pairs={{4,0},{8,4},{12,8},{16,12},{20,16},{24,20},{28,24},{0,28},{5,1},{9... | collective-permute-start | bytes 24584 | tf_op jit(solution)/shard_map/ppermute | solution.py:21
  87.9 9.4 %collective-permute-start.22 = (f32[2,8,34,1]{3,1,2,0:T(8,128)S(1)}, f32[2,8,34,1]{3,1,2,0:T(8,128)S(1)}, u32[]{:S(2)}, u32[]{:S(2)}) collective-permute-start(f32[2,8,34,1]{3,1,2,0:T(8,128)S(1)} %get-tuple-element.32), channel_id=1, source_target_pairs={{1,0},{2,1},{3,2},{0,3},{5,4},{6,5},{7,6},{4,7},{9,8},{10,9},{11,1... | collective-permute-start | bytes 6536 | tf_op jit(solution)/shard_map/ppermute | solution.py:21
  88.4 11.8 %collective-permute-start.23 = (f32[2,8,34,1]{3,1,2,0:T(8,128)S(1)}, f32[2,8,34,1]{3,1,2,0:T(8,128)S(1)}, u32[]{:S(2)}, u32[]{:S(2)}) collective-permute-start(f32[2,8,34,1]{3,1,2,0:T(8,128)S(1)} %get-tuple-element.31), channel_id=1, source_target_pairs={{0,1},{1,2},{2,3},{3,0},{4,5},{5,6},{6,7},{7,4},{8,9},{9,10},{10,1... | collective-permute-start | bytes 6536 | tf_op jit(solution)/shard_map/ppermute | solution.py:19
  105.5 5.1 %collective-permute-start.26 = (f32[1,8,34,1]{3,1,2,0:T(8,128)S(1)}, f32[1,8,34,1]{3,1,2,0:T(8,128)S(1)}, u32[]{:S(2)}, u32[]{:S(2)}) collective-permute-start(f32[1,8,34,1]{3,1,2,0:T(8,128)S(1)} %get-tuple-element.55), channel_id=1, source_target_pairs={{1,0},{2,1},{3,2},{0,3},{5,4},{6,5},{7,6},{4,7},{9,8},{10,9},{11,1... | collective-permute-start | bytes 3272 | tf_op jit(solution)/shard_map/ppermute | solution.py:21
  106.9 6.1 %collective-permute-start.27 = (f32[1,8,34,1]{3,1,2,0:T(8,128)S(1)}, f32[1,8,34,1]{3,1,2,0:T(8,128)S(1)}, u32[]{:S(2)}, u32[]{:S(2)}) collective-permute-start(f32[1,8,34,1]{3,1,2,0:T(8,128)S(1)} %get-tuple-element.56), channel_id=1, source_target_pairs={{0,1},{1,2},{2,3},{3,0},{4,5},{5,6},{6,7},{7,4},{8,9},{9,10},{10,1... | collective-permute-start | bytes 3272 | tf_op jit(solution)/shard_map/ppermute | solution.py:19
  113.2 4.9 %collective-permute-start.28 = (f32[2,8,1,128]{3,1,2,0:T(8,128)S(1)}, f32[2,8,1,128]{3,1,2,0:T(8,128)S(1)}, u32[]{:S(2)}, u32[]{:S(2)}) collective-permute-start(f32[2,8,1,128]{3,1,2,0:T(8,128)S(1)} %get-tuple-element.39), channel_id=1, source_target_pairs={{0,4},{4,8},{8,12},{12,16},{16,20},{20,24},{24,28},{28,0},{1,5},{5... | collective-permute-start | bytes 24584 | tf_op jit(solution)/shard_map/ppermute | solution.py:19
  118.3 9.6 %collective-permute-start.30 = (f32[2,8,34,1]{3,1,2,0:T(8,128)S(1)}, f32[2,8,34,1]{3,1,2,0:T(8,128)S(1)}, u32[]{:S(2)}, u32[]{:S(2)}) collective-permute-start(f32[2,8,34,1]{3,1,2,0:T(8,128)S(1)} %get-tuple-element.30), channel_id=1, source_target_pairs={{1,0},{2,1},{3,2},{0,3},{5,4},{6,5},{7,6},{4,7},{9,8},{10,9},{11,1... | collective-permute-start | bytes 6536 | tf_op jit(solution)/shard_map/ppermute | solution.py:21
  118.9 12.2 %collective-permute-start.31 = (f32[2,8,34,1]{3,1,2,0:T(8,128)S(1)}, f32[2,8,34,1]{3,1,2,0:T(8,128)S(1)}, u32[]{:S(2)}, u32[]{:S(2)}) collective-permute-start(f32[2,8,34,1]{3,1,2,0:T(8,128)S(1)} %get-tuple-element.29), channel_id=1, source_target_pairs={{0,1},{1,2},{2,3},{3,0},{4,5},{5,6},{6,7},{7,4},{8,9},{9,10},{10,1... | collective-permute-start | bytes 6536 | tf_op jit(solution)/shard_map/ppermute | solution.py:19
  147.2 9.2 %all-to-all-start.1 = ((bf16[4,8,1024]{2,0,1:T(4,128)(2,1)}), bf16[4,8,1024]{2,0,1:T(4,128)(2,1)S(1)}, u32[]{:S(2)}, u32[]{:S(2)}) async-start(bf16[4,8,1024]{2,0,1:T(4,128)(2,1)} %copy.39), calls=%async_computation.1 | async-start | bytes 131072 | tf_op jit(solution)/shard_map/all_to_all | solution.py:114
  157.1 14.8 %all-to-all-start.2 = ((bf16[4,8,1024]{2,1,0:T(8,128)(2,1)}), bf16[4,8,1024]{2,1,0:T(8,128)(2,1)S(1)}, u32[]{:S(2)}, u32[]{:S(2)}) async-start(bf16[4,8,1024]{2,1,0:T(8,128)(2,1)} %copy.40), calls=%async_computation.2 | async-start | bytes 131072 | tf_op jit(solution)/shard_map/all_to_all | solution.py:113
  193.2 8.8 %all-to-all-start.4 = ((bf16[4,8,1024]{2,1,0:T(8,128)(2,1)}), bf16[4,8,1024]{2,1,0:T(8,128)(2,1)S(1)}, u32[]{:S(2)}, u32[]{:S(2)}) async-start(bf16[4,8,1024]{2,1,0:T(8,128)(2,1)} %copy.44), calls=%async_computation.4 | async-start | bytes 131072 | tf_op jit(solution)/shard_map/all_to_all | solution.py:127
  226.0 6.5 %collective-permute-start.34 = (f32[1,8,34,1]{3,1,2,0:T(8,128)S(1)}, f32[1,8,34,1]{3,1,2,0:T(8,128)S(1)}, u32[]{:S(2)}, u32[]{:S(2)}) collective-permute-start(f32[1,8,34,1]{3,1,2,0:T(8,128)S(1)} %get-tuple-element.53), channel_id=1, source_target_pairs={{1,0},{2,1},{3,2},{0,3},{5,4},{6,5},{7,6},{4,7},{9,8},{10,9},{11,1... | collective-permute-start | bytes 3272 | tf_op jit(solution)/shard_map/ppermute | solution.py:21
  226.8 7.5 %collective-permute-start.35 = (f32[1,8,34,1]{3,1,2,0:T(8,128)S(1)}, f32[1,8,34,1]{3,1,2,0:T(8,128)S(1)}, u32[]{:S(2)}, u32[]{:S(2)}) collective-permute-start(f32[1,8,34,1]{3,1,2,0:T(8,128)S(1)} %get-tuple-element.54), channel_id=1, source_target_pairs={{0,1},{1,2},{2,3},{3,0},{4,5},{5,6},{6,7},{7,4},{8,9},{9,10},{10,1... | collective-permute-start | bytes 3272 | tf_op jit(solution)/shard_map/ppermute | solution.py:19
  234.5 4.9 %collective-permute-start.36 = (f32[2,8,1,128]{3,1,2,0:T(8,128)S(1)}, f32[2,8,1,128]{3,1,2,0:T(8,128)S(1)}, u32[]{:S(2)}, u32[]{:S(2)}) collective-permute-start(f32[2,8,1,128]{3,1,2,0:T(8,128)S(1)} %get-tuple-element.37), channel_id=1, source_target_pairs={{0,4},{4,8},{8,12},{12,16},{16,20},{20,24},{24,28},{28,0},{1,5},{5... | collective-permute-start | bytes 24584 | tf_op jit(solution)/shard_map/ppermute | solution.py:19
  239.6 9.6 %collective-permute-start.38 = (f32[2,8,34,1]{3,1,2,0:T(8,128)S(1)}, f32[2,8,34,1]{3,1,2,0:T(8,128)S(1)}, u32[]{:S(2)}, u32[]{:S(2)}) collective-permute-start(f32[2,8,34,1]{3,1,2,0:T(8,128)S(1)} %get-tuple-element.28), channel_id=1, source_target_pairs={{1,0},{2,1},{3,2},{0,3},{5,4},{6,5},{7,6},{4,7},{9,8},{10,9},{11,1... | collective-permute-start | bytes 6536 | tf_op jit(solution)/shard_map/ppermute | solution.py:21
  241.1 11.9 %collective-permute-start.39 = (f32[2,8,34,1]{3,1,2,0:T(8,128)S(1)}, f32[2,8,34,1]{3,1,2,0:T(8,128)S(1)}, u32[]{:S(2)}, u32[]{:S(2)}) collective-permute-start(f32[2,8,34,1]{3,1,2,0:T(8,128)S(1)} %get-tuple-element.27), channel_id=1, source_target_pairs={{0,1},{1,2},{2,3},{3,0},{4,5},{5,6},{6,7},{7,4},{8,9},{9,10},{10,1... | collective-permute-start | bytes 6536 | tf_op jit(solution)/shard_map/ppermute | solution.py:19
  (14 other events, 188.9 us)
where the time goes:
time: 255 us; the launch traced here: 254 us
  waiting for transfers between devices  106 us (42%)
  starting transfers between devices  69.7 us (27%)
  local copies, waits for them, and re-layouts  29.8 us (12%)
  blocking collectives  23.4 us (9%)
  matrix products  16.7 us (7%)
  other arithmetic  7.33 us (3%)
    ppermute x20, waiting for transfers between devices, with_halo(): lax.ppermute(head, axis, [((i + 1) % count, i) for i in range(count)])  53.3 us
    ppermute x20, starting transfers between devices, with_halo(): lax.ppermute(head, axis, [((i + 1) % count, i) for i in range(count)])  50.4 us
    ppermute x20, waiting for transfers between devices, with_halo(): lax.ppermute(tail, axis, [(i, (i + 1) % count) for i in range(count)])  41.6 us
    gather x24, local copies, waits for them, and re-layouts  11 us
    ppermute x20, starting transfers between devices, with_halo(): lax.ppermute(tail, axis, [(i, (i + 1) % count) for i in range(count)])  8.48 us
    all_to_all x1, blocking collectives, local(): lax.all_to_all(arranged, 'lat', split_axis=1, concat_axis=1, tiled=True)  8.3 us
    all_to_all x1, blocking collectives, local(): lax.all_to_all(height, 'lon', split_axis=1, concat_axis=2, tiled=True)  7.73 us
    all_to_all x1, blocking collectives, local(): lax.all_to_all(grid_rows, 'lon', split_axis=2, concat_axis=1, tiled=True)  7.41 us
  transfers between devices with their start and end apart: 43, of which 33 were waited for; matrix products, arithmetic and copies ran while one was open for 5% of the time, Pallas kernels for 0%

commit v1 on v0

--- a/solution.py
+++ b/solution.py
@@ -138,7 +138,19 @@
     ) - jnp.einsum(
         "mx,mfr->frx", sin_full * doubling[:, None], returned[:, 1], precision=exact_mode
     )
-    loading = lax.all_to_all(grid_rows, "lon", split_axis=2, concat_axis=1, tiled=True)
+
+    def wait_ranges_by_axis(block_here):
+        return jnp.concatenate(
+            jax.lax.all_to_all(
+                jnp.stack(jnp.split(block_here, jax.lax.axis_size("lon"), 2)),
+                "lon",
+                split_axis=0,
+                concat_axis=0,
+            ),
+            1,
+        )
+
+    loading = wait_ranges_by_axis(grid_rows)
     height = height + wetness * loading
     return advance(height, east_flow, north_flow)
 

time: 255 us -> 266 us (1.043)
  waiting for transfers between devices: 106 us -> 123 us
  local copies, waits for them, and re-layouts: 29.8 us -> 24 us
    ppermute x20, waiting for transfers between devices: 53.3 us -> 63.8 us  [with_halo(): lax.ppermute(head, axis, [((i + 1) % count, i) for i in range(count)])]
    ppermute x20, waiting for transfers between devices: 41.6 us -> 48.2 us  [with_halo(): lax.ppermute(tail, axis, [(i, (i + 1) % count) for i in range(count)])]
    unnamed x13 -> x14, local copies, waits for them, and re-layouts: 4.86 us -> 0.65 us
where the time goes in v1:
time: 266 us; the launch traced here: 265 us
  waiting for transfers between devices  123 us (46%)
  starting transfers between devices  70 us (26%)
  local copies, waits for them, and re-layouts  24 us (9%)
  blocking collectives  23.8 us (9%)
  matrix products  16.7 us (6%)
  other arithmetic  6.66 us (3%)
    ppermute x20, waiting for transfers between devices, with_halo(): lax.ppermute(head, axis, [((i + 1) % count, i) for i in range(count)])  63.8 us
    ppermute x20, starting transfers between devices, with_halo(): lax.ppermute(head, axis, [((i + 1) % count, i) for i in range(count)])  52.5 us
    ppermute x20, waiting for transfers between devices, with_halo(): lax.ppermute(tail, axis, [(i, (i + 1) % count) for i in range(count)])  48.2 us
    gather x24, local copies, waits for them, and re-layouts  11 us
    all_to_all x1, blocking collectives, local(): lax.all_to_all(arranged, 'lat', split_axis=1, concat_axis=1, tiled=True)  8.3 us
    all_to_all x1, blocking collectives, local(): lax.all_to_all(height, 'lon', split_axis=1, concat_axis=2, tiled=True)  8.06 us
    all_to_all x1, blocking collectives, wait_ranges_by_axis(): jax.lax.all_to_all(jnp.stack(jnp.split(block_here, jax.lax.axis_size('lon...  7.41 us
    dot_general x1, matrix products, spherical(): jnp.einsum('kcn,kirn->kicr', coefficients, legendre_blocks, preferred_ele...  7.06 us
  transfers between devices with their start and end apart: 43, of which 33 were waited for; matrix products, arithmetic and copies ran while one was open for 5% of the time, Pallas kernels for 0%

profile of v1, /device:TPU:0, one launch (start us, length us, event | category | flops | bytes accessed | tf_op | source)
XLA Modules:
  0.0 265.1 jit_solution(13085371641310010426)
XLA Ops:
  2.9 4.1 %collective-permute-start.1 = (f32[1,8,1,128]{3,2,1,0:T(1,128)S(1)}, f32[1,8,1,128]{3,2,1,0:T(1,128)S(1)}, u32[]{:S(2)}, u32[]{:S(2)}) collective-permute-start(f32[1,8,1,128]{3,2,1,0:T(1,128)S(1)} %get-tuple-element.69), channel_id=1, source_target_pairs={{4,0},{8,4},{12,8},{16,12},{20,16},{24,20},{28,24},{0,28},{5,1},{9... | collective-permute-start | bytes 12296 | tf_op jit(solution)/shard_map/ppermute | solution.py:21
  12.1 3.9 %collective-permute-done.2 = f32[1,8,34,1]{3,2,1,0:T(8,128)S(1)} collective-permute-done((f32[1,8,34,1]{3,2,1,0:T(8,128)S(1)}, f32[1,8,34,1]{3,2,1,0:T(8,128)S(1)}, u32[]{:S(2)}, u32[]{:S(2)}) %collective-permute-start.2) | collective-permute-done | bytes 1120 | tf_op jit(solution)/shard_map/ppermute | solution.py:21
  16.0 3.6 %collective-permute-done.3 = f32[1,8,34,1]{3,2,1,0:T(8,128)S(1)} collective-permute-done((f32[1,8,34,1]{3,2,1,0:T(8,128)S(1)}, f32[1,8,34,1]{3,2,1,0:T(8,128)S(1)}, u32[]{:S(2)}, u32[]{:S(2)}) %collective-permute-start.3) | collective-permute-done | bytes 1120 | tf_op jit(solution)/shard_map/ppermute | solution.py:19
  20.8 3.5 %collective-permute-start.5 = (f32[2,8,1,128]{3,2,1,0:T(1,128)S(1)}, f32[2,8,1,128]{3,2,1,0:T(1,128)S(1)}, u32[]{:S(2)}, u32[]{:S(2)}) collective-permute-start(f32[2,8,1,128]{3,2,1,0:T(1,128)S(1)} %get-tuple-element.40), channel_id=1, source_target_pairs={{4,0},{8,4},{12,8},{16,12},{20,16},{24,20},{28,24},{0,28},{5,1},{9... | collective-permute-start | bytes 24584 | tf_op jit(solution)/shard_map/ppermute | solution.py:21
  28.0 8.6 %collective-permute-done.6 = f32[2,8,34,1]{3,2,1,0:T(8,128)S(1)} collective-permute-done((f32[2,8,34,1]{3,2,1,0:T(8,128)S(1)}, f32[2,8,34,1]{3,2,1,0:T(8,128)S(1)}, u32[]{:S(2)}, u32[]{:S(2)}) %collective-permute-start.6) | collective-permute-done | bytes 2208 | tf_op jit(solution)/shard_map/ppermute | solution.py:21
  36.6 4.3 %collective-permute-done.7 = f32[2,8,34,1]{3,2,1,0:T(8,128)S(1)} collective-permute-done((f32[2,8,34,1]{3,2,1,0:T(8,128)S(1)}, f32[2,8,34,1]{3,2,1,0:T(8,128)S(1)}, u32[]{:S(2)}, u32[]{:S(2)}) %collective-permute-start.7) | collective-permute-done | bytes 2208 | tf_op jit(solution)/shard_map/ppermute | solution.py:19
  41.1 3.5 %collective-permute-start.9 = (f32[1,8,1,128]{3,2,1,0:T(1,128)S(1)}, f32[1,8,1,128]{3,2,1,0:T(1,128)S(1)}, u32[]{:S(2)}, u32[]{:S(2)}) collective-permute-start(f32[1,8,1,128]{3,2,1,0:T(1,128)S(1)} %get-tuple-element.67), channel_id=1, source_target_pairs={{4,0},{8,4},{12,8},{16,12},{20,16},{24,20},{28,24},{0,28},{5,1},{9... | collective-permute-start | bytes 12296 | tf_op jit(solution)/shard_map/ppermute | solution.py:21
  48.6 4.2 %collective-permute-done.10 = f32[1,8,34,1]{3,2,1,0:T(8,128)S(1)} collective-permute-done((f32[1,8,34,1]{3,2,1,0:T(8,128)S(1)}, f32[1,8,34,1]{3,2,1,0:T(8,128)S(1)}, u32[]{:S(2)}, u32[]{:S(2)}) %collective-permute-start.10) | collective-permute-done | bytes 1120 | tf_op jit(solution)/shard_map/ppermute | solution.py:21
  55.8 3.5 %collective-permute-start.13 = (f32[2,8,1,128]{3,2,1,0:T(1,128)S(1)}, f32[2,8,1,128]{3,2,1,0:T(1,128)S(1)}, u32[]{:S(2)}, u32[]{:S(2)}) collective-permute-start(f32[2,8,1,128]{3,2,1,0:T(1,128)S(1)} %get-tuple-element.38), channel_id=1, source_target_pairs={{4,0},{8,4},{12,8},{16,12},{20,16},{24,20},{28,24},{0,28},{5,1},{9... | collective-permute-start | bytes 24584 | tf_op jit(solution)/shard_map/ppermute | solution.py:21
  63.0 8.6 %collective-permute-done.14 = f32[2,8,34,1]{3,2,1,0:T(8,128)S(1)} collective-permute-done((f32[2,8,34,1]{3,2,1,0:T(8,128)S(1)}, f32[2,8,34,1]{3,2,1,0:T(8,128)S(1)}, u32[]{:S(2)}, u32[]{:S(2)}) %collective-permute-start.14) | collective-permute-done | bytes 2208 | tf_op jit(solution)/shard_map/ppermute | solution.py:21
  71.6 3.9 %collective-permute-done.15 = f32[2,8,34,1]{3,2,1,0:T(8,128)S(1)} collective-permute-done((f32[2,8,34,1]{3,2,1,0:T(8,128)S(1)}, f32[2,8,34,1]{3,2,1,0:T(8,128)S(1)}, u32[]{:S(2)}, u32[]{:S(2)}) %collective-permute-start.15) | collective-permute-done | bytes 2208 | tf_op jit(solution)/shard_map/ppermute | solution.py:19
  75.8 3.5 %collective-permute-start.17 = (f32[1,8,1,128]{3,2,1,0:T(1,128)S(1)}, f32[1,8,1,128]{3,2,1,0:T(1,128)S(1)}, u32[]{:S(2)}, u32[]{:S(2)}) collective-permute-start(f32[1,8,1,128]{3,2,1,0:T(1,128)S(1)} %get-tuple-element.65), channel_id=1, source_target_pairs={{4,0},{8,4},{12,8},{16,12},{20,16},{24,20},{28,24},{0,28},{5,1},{9... | collective-permute-start | bytes 12296 | tf_op jit(solution)/shard_map/ppermute | solution.py:21
  83.1 3.5 %collective-permute-done.18 = f32[1,8,34,1]{3,2,1,0:T(8,128)S(1)} collective-permute-done((f32[1,8,34,1]{3,2,1,0:T(8,128)S(1)}, f32[1,8,34,1]{3,2,1,0:T(8,128)S(1)}, u32[]{:S(2)}, u32[]{:S(2)}) %collective-permute-start.18) | collective-permute-done | bytes 1120 | tf_op jit(solution)/shard_map/ppermute | solution.py:21
  96.7 8.6 %collective-permute-done.22 = f32[2,8,34,1]{3,2,1,0:T(8,128)S(1)} collective-permute-done((f32[2,8,34,1]{3,2,1,0:T(8,128)S(1)}, f32[2,8,34,1]{3,2,1,0:T(8,128)S(1)}, u32[]{:S(2)}, u32[]{:S(2)}) %collective-permute-start.22) | collective-permute-done | bytes 2208 | tf_op jit(solution)/shard_map/ppermute | solution.py:21
  105.3 3.9 %collective-permute-done.23 = f32[2,8,34,1]{3,2,1,0:T(8,128)S(1)} collective-permute-done((f32[2,8,34,1]{3,2,1,0:T(8,128)S(1)}, f32[2,8,34,1]{3,2,1,0:T(8,128)S(1)}, u32[]{:S(2)}, u32[]{:S(2)}) %collective-permute-start.23) | collective-permute-done | bytes 2208 | tf_op jit(solution)/shard_map/ppermute | solution.py:19
  109.5 3.5 %collective-permute-start.25 = (f32[1,8,1,128]{3,2,1,0:T(1,128)S(1)}, f32[1,8,1,128]{3,2,1,0:T(1,128)S(1)}, u32[]{:S(2)}, u32[]{:S(2)}) collective-permute-start(f32[1,8,1,128]{3,2,1,0:T(1,128)S(1)} %get-tuple-element.63), channel_id=1, source_target_pairs={{4,0},{8,4},{12,8},{16,12},{20,16},{24,20},{28,24},{0,28},{5,1},{9... | collective-permute-start | bytes 12296 | tf_op jit(solution)/shard_map/ppermute | solution.py:21
  116.6 4.1 %collective-permute-done.26 = f32[1,8,34,1]{3,2,1,0:T(8,128)S(1)} collective-permute-done((f32[1,8,34,1]{3,2,1,0:T(8,128)S(1)}, f32[1,8,34,1]{3,2,1,0:T(8,128)S(1)}, u32[]{:S(2)}, u32[]{:S(2)}) %collective-permute-start.26) | collective-permute-done | bytes 1120 | tf_op jit(solution)/shard_map/ppermute | solution.py:21
  123.6 3.5 %collective-permute-start.29 = (f32[2,8,1,128]{3,2,1,0:T(1,128)S(1)}, f32[2,8,1,128]{3,2,1,0:T(1,128)S(1)}, u32[]{:S(2)}, u32[]{:S(2)}) collective-permute-start(f32[2,8,1,128]{3,2,1,0:T(1,128)S(1)} %get-tuple-element.34), channel_id=1, source_target_pairs={{4,0},{8,4},{12,8},{16,12},{20,16},{24,20},{28,24},{0,28},{5,1},{9... | collective-permute-start | bytes 24584 | tf_op jit(solution)/shard_map/ppermute | solution.py:21
  130.9 8.6 %collective-permute-done.30 = f32[2,8,34,1]{3,2,1,0:T(8,128)S(1)} collective-permute-done((f32[2,8,34,1]{3,2,1,0:T(8,128)S(1)}, f32[2,8,34,1]{3,2,1,0:T(8,128)S(1)}, u32[]{:S(2)}, u32[]{:S(2)}) %collective-permute-start.30) | collective-permute-done | bytes 2208 | tf_op jit(solution)/shard_map/ppermute | solution.py:21
  139.4 4.3 %collective-permute-done.31 = f32[2,8,34,1]{3,2,1,0:T(8,128)S(1)} collective-permute-done((f32[2,8,34,1]{3,2,1,0:T(8,128)S(1)}, f32[2,8,34,1]{3,2,1,0:T(8,128)S(1)}, u32[]{:S(2)}, u32[]{:S(2)}) %collective-permute-start.31) | collective-permute-done | bytes 2208 | tf_op jit(solution)/shard_map/ppermute | solution.py:19
  144.0 8.1 %all_to_all.43 = f32[8,32,128]{2,0,1:T(8,128)S(1)} all-to-all(f32[8,32,128]{2,0,1:T(8,128)S(1)} %copy.29), channel_id=1, replica_groups=mesh['lat'=8,'lon'=4] {'lon'}, dimensions={1} | all-to-all | bytes 262144 | tf_op jit(solution)/shard_map/all_to_all | solution.py:108
  163.6 5.8 %all-to-all-done.1 = bf16[4,8,1024]{2,0,1:T(4,128)(2,1)S(1)} async-done(((bf16[4,8,1024]{2,0,1:T(4,128)(2,1)}), bf16[4,8,1024]{2,0,1:T(4,128)(2,1)S(1)}, u32[]{:S(2)}, u32[]{:S(2)}) %all-to-all-start.1) | async-done | bytes 65568 | tf_op jit(solution)/shard_map/all_to_all | solution.py:114
  173.7 11.2 %while.1 = (s32[]{:T(128)}, f32[1280]{0:T(1024)S(1)}, s32[8,1]{0,1:T(1,128)S(1)}, f32[8,1024]{1,0:T(8,128)S(1)}, s32[]{:T(128)}, /*index=5*/s32[]{:T(128)}) while((s32[]{:T(128)}, f32[1280]{0:T(1024)S(1)}, s32[8,1]{0,1:T(1,128)S(1)}, f32[8,1024]{1,0:T(8,128)S(1)}, s32[]{:T(128)}, /*index=5*/s32[]{:T(128)}) %tuple.47), condition=%wide.while_cond, body=%wide.while_body.sunk | while | flops 2 | bytes 16473 | solution.py:104
  188.0 7.1 %fusion.3 = bf16[8,8,16,32]{3,2,1,0:T(8,128)(2,1)S(1)} fusion(bf16[8,8,32,1024]{3,2,1,0:T(8,128)(2,1)} %bitcast.223, bf16[8,8,16,32]{3,2,1,0:T(8,128)(2,1)S(1)} %reshape_reshape.3, f32[8,1024]{1,0:T(8,128)S(1)} %get-tuple-element.10), kind=kOutput, calls=%fused_computation.6 | convolution fusion | flops 134512640 | bytes 4358144 | tf_op jit(solution)/shard_map/kcn,kirn->kicr/dot_general | solution.py:63
  197.2 8.3 %all_to_all.44 = bf16[4,8,1024]{2,0,1:T(4,128)(2,1)S(1)} all-to-all(bf16[4,8,1024]{2,0,1:T(4,128)(2,1)S(1)} %copy.36), channel_id=1, replica_groups=mesh['lat'=8,'lon'=4] {'lat'}, dimensions={1} | all-to-all | bytes 131072 | tf_op jit(solution)/shard_map/all_to_all | solution.py:128
  206.2 3.9 %all-to-all-start.4 = ((bf16[4,8,1024]{2,1,0:T(8,128)(2,1)}), bf16[4,8,1024]{2,1,0:T(8,128)(2,1)S(1)}, u32[]{:S(2)}, u32[]{:S(2)}) async-start(bf16[4,8,1024]{2,1,0:T(8,128)(2,1)} %copy.37), calls=%async_computation.4 | async-start | bytes 131072 | tf_op jit(solution)/shard_map/all_to_all | solution.py:127
  210.1 4.8 %all-to-all-done.4 = bf16[4,8,1024]{2,1,0:T(8,128)(2,1)S(1)} async-done(((bf16[4,8,1024]{2,1,0:T(8,128)(2,1)}), bf16[4,8,1024]{2,1,0:T(8,128)(2,1)S(1)}, u32[]{:S(2)}, u32[]{:S(2)}) %all-to-all-start.4) | async-done | bytes 65568 | tf_op jit(solution)/shard_map/all_to_all | solution.py:127
  221.5 7.4 %all_to_all.45 = f32[4,8,8,128]{3,2,1,0:T(8,128)S(1)} all-to-all(f32[4,8,8,128]{3,2,1,0:T(8,128)S(1)} %pad_maximum_fusion.110), channel_id=1, replica_groups=mesh['lat'=8,'lon'=4] {'lon'}, dimensions={0} | all-to-all | bytes 262144 | tf_op jit(solution)/shard_map/all_to_all | solution.py:144
  229.0 3.5 %collective-permute-start.33 = (f32[1,8,1,128]{3,2,1,0:T(1,128)S(1)}, f32[1,8,1,128]{3,2,1,0:T(1,128)S(1)}, u32[]{:S(2)}, u32[]{:S(2)}) collective-permute-start(f32[1,8,1,128]{3,2,1,0:T(1,128)S(1)} %get-tuple-element.57), channel_id=1, source_target_pairs={{4,0},{8,4},{12,8},{16,12},{20,16},{24,20},{28,24},{0,28},{5,1},{9... | collective-permute-start | bytes 12296 | tf_op jit(solution)/shard_map/ppermute | solution.py:21
  236.2 4.9 %collective-permute-done.34 = f32[1,8,34,1]{3,2,1,0:T(8,128)S(1)} collective-permute-done((f32[1,8,34,1]{3,2,1,0:T(8,128)S(1)}, f32[1,8,34,1]{3,2,1,0:T(8,128)S(1)}, u32[]{:S(2)}, u32[]{:S(2)}) %collective-permute-start.34) | collective-permute-done | bytes 1120 | tf_op jit(solution)/shard_map/ppermute | solution.py:21
  250.8 8.6 %collective-permute-done.38 = f32[2,8,34,1]{3,2,1,0:T(8,128)S(1)} collective-permute-done((f32[2,8,34,1]{3,2,1,0:T(8,128)S(1)}, f32[2,8,34,1]{3,2,1,0:T(8,128)S(1)}, u32[]{:S(2)}, u32[]{:S(2)}) %collective-permute-start.38) | collective-permute-done | bytes 2208 | tf_op jit(solution)/shard_map/ppermute | solution.py:21
  259.4 4.9 %collective-permute-done.39 = f32[2,8,34,1]{3,2,1,0:T(8,128)S(1)} collective-permute-done((f32[2,8,34,1]{3,2,1,0:T(8,128)S(1)}, f32[2,8,34,1]{3,2,1,0:T(8,128)S(1)}, u32[]{:S(2)}, u32[]{:S(2)}) %collective-permute-start.39) | collective-permute-done | bytes 2208 | tf_op jit(solution)/shard_map/ppermute | solution.py:19
  (170 shorter events, 101.3 us)
Async XLA Ops:
  2.3 5.9 %collective-permute-start = (f32[1,8,1,128]{3,2,1,0:T(1,128)S(1)}, f32[1,8,1,128]{3,2,1,0:T(1,128)S(1)}, u32[]{:S(2)}, u32[]{:S(2)}) collective-permute-start(f32[1,8,1,128]{3,2,1,0:T(1,128)S(1)} %get-tuple-element.70), channel_id=1, source_target_pairs={{0,4},{4,8},{8,12},{12,16},{16,20},{20,24},{24,28},{28,0},{1,5},{5... | collective-permute-start | bytes 12296 | tf_op jit(solution)/shard_map/ppermute | solution.py:19
  2.9 5.4 %collective-permute-start.1 = (f32[1,8,1,128]{3,2,1,0:T(1,128)S(1)}, f32[1,8,1,128]{3,2,1,0:T(1,128)S(1)}, u32[]{:S(2)}, u32[]{:S(2)}) collective-permute-start(f32[1,8,1,128]{3,2,1,0:T(1,128)S(1)} %get-tuple-element.69), channel_id=1, source_target_pairs={{4,0},{8,4},{12,8},{16,12},{20,16},{24,20},{28,24},{0,28},{5,1},{9... | collective-permute-start | bytes 12296 | tf_op jit(solution)/shard_map/ppermute | solution.py:21
  8.4 7.5 %collective-permute-start.2 = (f32[1,8,34,1]{3,2,1,0:T(8,128)S(1)}, f32[1,8,34,1]{3,2,1,0:T(8,128)S(1)}, u32[]{:S(2)}, u32[]{:S(2)}) collective-permute-start(f32[1,8,34,1]{3,2,1,0:T(8,128)S(1)} %get-tuple-element.55), channel_id=1, source_target_pairs={{1,0},{2,1},{3,2},{0,3},{5,4},{6,5},{7,6},{4,7},{9,8},{10,9},{11,1... | collective-permute-start | bytes 3272 | tf_op jit(solution)/shard_map/ppermute | solution.py:21
  11.4 8.2 %collective-permute-start.3 = (f32[1,8,34,1]{3,2,1,0:T(8,128)S(1)}, f32[1,8,34,1]{3,2,1,0:T(8,128)S(1)}, u32[]{:S(2)}, u32[]{:S(2)}) collective-permute-start(f32[1,8,34,1]{3,2,1,0:T(8,128)S(1)} %get-tuple-element.56), channel_id=1, source_target_pairs={{0,1},{1,2},{2,3},{3,0},{4,5},{5,6},{6,7},{7,4},{8,9},{9,10},{10,1... | collective-permute-start | bytes 3272 | tf_op jit(solution)/shard_map/ppermute | solution.py:19
  20.8 4.9 %collective-permute-start.4 = (f32[2,8,1,128]{3,2,1,0:T(1,128)S(1)}, f32[2,8,1,128]{3,2,1,0:T(1,128)S(1)}, u32[]{:S(2)}, u32[]{:S(2)}) collective-permute-start(f32[2,8,1,128]{3,2,1,0:T(1,128)S(1)} %get-tuple-element.39), channel_id=1, source_target_pairs={{0,4},{4,8},{8,12},{12,16},{16,20},{20,24},{24,28},{28,0},{1,5},{5... | collective-permute-start | bytes 24584 | tf_op jit(solution)/shard_map/ppermute | solution.py:19
  20.8 4.9 %collective-permute-start.5 = (f32[2,8,1,128]{3,2,1,0:T(1,128)S(1)}, f32[2,8,1,128]{3,2,1,0:T(1,128)S(1)}, u32[]{:S(2)}, u32[]{:S(2)}) collective-permute-start(f32[2,8,1,128]{3,2,1,0:T(1,128)S(1)} %get-tuple-element.40), channel_id=1, source_target_pairs={{4,0},{8,4},{12,8},{16,12},{20,16},{24,20},{28,24},{0,28},{5,1},{9... | collective-permute-start | bytes 24584 | tf_op jit(solution)/shard_map/ppermute | solution.py:21
  25.9 10.6 %collective-permute-start.6 = (f32[2,8,34,1]{3,2,1,0:T(8,128)S(1)}, f32[2,8,34,1]{3,2,1,0:T(8,128)S(1)}, u32[]{:S(2)}, u32[]{:S(2)}) collective-permute-start(f32[2,8,34,1]{3,2,1,0:T(8,128)S(1)} %get-tuple-element.30), channel_id=1, source_target_pairs={{1,0},{2,1},{3,2},{0,3},{5,4},{6,5},{7,6},{4,7},{9,8},{10,9},{11,1... | collective-permute-start | bytes 6536 | tf_op jit(solution)/shard_map/ppermute | solution.py:21
  27.4 13.4 %collective-permute-start.7 = (f32[2,8,34,1]{3,2,1,0:T(8,128)S(1)}, f32[2,8,34,1]{3,2,1,0:T(8,128)S(1)}, u32[]{:S(2)}, u32[]{:S(2)}) collective-permute-start(f32[2,8,34,1]{3,2,1,0:T(8,128)S(1)} %get-tuple-element.29), channel_id=1, source_target_pairs={{0,1},{1,2},{2,3},{3,0},{4,5},{5,6},{6,7},{7,4},{8,9},{9,10},{10,1... | collective-permute-start | bytes 6536 | tf_op jit(solution)/shard_map/ppermute | solution.py:19
  46.1 6.7 %collective-permute-start.10 = (f32[1,8,34,1]{3,2,1,0:T(8,128)S(1)}, f32[1,8,34,1]{3,2,1,0:T(8,128)S(1)}, u32[]{:S(2)}, u32[]{:S(2)}) collective-permute-start(f32[1,8,34,1]{3,2,1,0:T(8,128)S(1)} %get-tuple-element.53), channel_id=1, source_target_pairs={{1,0},{2,1},{3,2},{0,3},{5,4},{6,5},{7,6},{4,7},{9,8},{10,9},{11,1... | collective-permute-start | bytes 3272 | tf_op jit(solution)/shard_map/ppermute | solution.py:21
  48.6 6.9 %collective-permute-start.11 = (f32[1,8,34,1]{3,2,1,0:T(8,128)S(1)}, f32[1,8,34,1]{3,2,1,0:T(8,128)S(1)}, u32[]{:S(2)}, u32[]{:S(2)}) collective-permute-start(f32[1,8,34,1]{3,2,1,0:T(8,128)S(1)} %get-tuple-element.54), channel_id=1, source_target_pairs={{0,1},{1,2},{2,3},{3,0},{4,5},{5,6},{6,7},{7,4},{8,9},{9,10},{10,1... | collective-permute-start | bytes 3272 | tf_op jit(solution)/shard_map/ppermute | solution.py:19
  55.8 4.9 %collective-permute-start.12 = (f32[2,8,1,128]{3,2,1,0:T(1,128)S(1)}, f32[2,8,1,128]{3,2,1,0:T(1,128)S(1)}, u32[]{:S(2)}, u32[]{:S(2)}) collective-permute-start(f32[2,8,1,128]{3,2,1,0:T(1,128)S(1)} %get-tuple-element.37), channel_id=1, source_target_pairs={{0,4},{4,8},{8,12},{12,16},{16,20},{20,24},{24,28},{28,0},{1,5},{5... | collective-permute-start | bytes 24584 | tf_op jit(solution)/shard_map/ppermute | solution.py:19
  60.9 10.6 %collective-permute-start.14 = (f32[2,8,34,1]{3,2,1,0:T(8,128)S(1)}, f32[2,8,34,1]{3,2,1,0:T(8,128)S(1)}, u32[]{:S(2)}, u32[]{:S(2)}) collective-permute-start(f32[2,8,34,1]{3,2,1,0:T(8,128)S(1)} %get-tuple-element.28), channel_id=1, source_target_pairs={{1,0},{2,1},{3,2},{0,3},{5,4},{6,5},{7,6},{4,7},{9,8},{10,9},{11,1... | collective-permute-start | bytes 6536 | tf_op jit(solution)/shard_map/ppermute | solution.py:21
  62.1 13.4 %collective-permute-start.15 = (f32[2,8,34,1]{3,2,1,0:T(8,128)S(1)}, f32[2,8,34,1]{3,2,1,0:T(8,128)S(1)}, u32[]{:S(2)}, u32[]{:S(2)}) collective-permute-start(f32[2,8,34,1]{3,2,1,0:T(8,128)S(1)} %get-tuple-element.27), channel_id=1, source_target_pairs={{0,1},{1,2},{2,3},{3,0},{4,5},{5,6},{6,7},{7,4},{8,9},{9,10},{10,1... | collective-permute-start | bytes 6536 | tf_op jit(solution)/shard_map/ppermute | solution.py:19
  80.8 5.9 %collective-permute-start.18 = (f32[1,8,34,1]{3,2,1,0:T(8,128)S(1)}, f32[1,8,34,1]{3,2,1,0:T(8,128)S(1)}, u32[]{:S(2)}, u32[]{:S(2)}) collective-permute-start(f32[1,8,34,1]{3,2,1,0:T(8,128)S(1)} %get-tuple-element.51), channel_id=1, source_target_pairs={{1,0},{2,1},{3,2},{0,3},{5,4},{6,5},{7,6},{4,7},{9,8},{10,9},{11,1... | collective-permute-start | bytes 3272 | tf_op jit(solution)/shard_map/ppermute | solution.py:21
  83.0 6.2 %collective-permute-start.19 = (f32[1,8,34,1]{3,2,1,0:T(8,128)S(1)}, f32[1,8,34,1]{3,2,1,0:T(8,128)S(1)}, u32[]{:S(2)}, u32[]{:S(2)}) collective-permute-start(f32[1,8,34,1]{3,2,1,0:T(8,128)S(1)} %get-tuple-element.52), channel_id=1, source_target_pairs={{0,1},{1,2},{2,3},{3,0},{4,5},{5,6},{6,7},{7,4},{8,9},{9,10},{10,1... | collective-permute-start | bytes 3272 | tf_op jit(solution)/shard_map/ppermute | solution.py:19
  89.5 4.9 %collective-permute-start.20 = (f32[2,8,1,128]{3,2,1,0:T(1,128)S(1)}, f32[2,8,1,128]{3,2,1,0:T(1,128)S(1)}, u32[]{:S(2)}, u32[]{:S(2)}) collective-permute-start(f32[2,8,1,128]{3,2,1,0:T(1,128)S(1)} %get-tuple-element.35), channel_id=1, source_target_pairs={{0,4},{4,8},{8,12},{12,16},{16,20},{20,24},{24,28},{28,0},{1,5},{5... | collective-permute-start | bytes 24584 | tf_op jit(solution)/shard_map/ppermute | solution.py:19
  94.7 10.6 %collective-permute-start.22 = (f32[2,8,34,1]{3,2,1,0:T(8,128)S(1)}, f32[2,8,34,1]{3,2,1,0:T(8,128)S(1)}, u32[]{:S(2)}, u32[]{:S(2)}) collective-permute-start(f32[2,8,34,1]{3,2,1,0:T(8,128)S(1)} %get-tuple-element.26), channel_id=1, source_target_pairs={{1,0},{2,1},{3,2},{0,3},{5,4},{6,5},{7,6},{4,7},{9,8},{10,9},{11,1... | collective-permute-start | bytes 6536 | tf_op jit(solution)/shard_map/ppermute | solution.py:21
  95.7 13.5 %collective-permute-start.23 = (f32[2,8,34,1]{3,2,1,0:T(8,128)S(1)}, f32[2,8,34,1]{3,2,1,0:T(8,128)S(1)}, u32[]{:S(2)}, u32[]{:S(2)}) collective-permute-start(f32[2,8,34,1]{3,2,1,0:T(8,128)S(1)} %get-tuple-element.25), channel_id=1, source_target_pairs={{0,1},{1,2},{2,3},{3,0},{4,5},{5,6},{6,7},{7,4},{8,9},{9,10},{10,1... | collective-permute-start | bytes 6536 | tf_op jit(solution)/shard_map/ppermute | solution.py:19
  114.5 6.2 %collective-permute-start.26 = (f32[1,8,34,1]{3,2,1,0:T(8,128)S(1)}, f32[1,8,34,1]{3,2,1,0:T(8,128)S(1)}, u32[]{:S(2)}, u32[]{:S(2)}) collective-permute-start(f32[1,8,34,1]{3,2,1,0:T(8,128)S(1)} %get-tuple-element.49), channel_id=1, source_target_pairs={{1,0},{2,1},{3,2},{0,3},{5,4},{6,5},{7,6},{4,7},{9,8},{10,9},{11,1... | collective-permute-start | bytes 3272 | tf_op jit(solution)/shard_map/ppermute | solution.py:21
  116.4 6.9 %collective-permute-start.27 = (f32[1,8,34,1]{3,2,1,0:T(8,128)S(1)}, f32[1,8,34,1]{3,2,1,0:T(8,128)S(1)}, u32[]{:S(2)}, u32[]{:S(2)}) collective-permute-start(f32[1,8,34,1]{3,2,1,0:T(8,128)S(1)} %get-tuple-element.50), channel_id=1, source_target_pairs={{0,1},{1,2},{2,3},{3,0},{4,5},{5,6},{6,7},{7,4},{8,9},{9,10},{10,1... | collective-permute-start | bytes 3272 | tf_op jit(solution)/shard_map/ppermute | solution.py:19
  123.6 5.0 %collective-permute-start.28 = (f32[2,8,1,128]{3,2,1,0:T(1,128)S(1)}, f32[2,8,1,128]{3,2,1,0:T(1,128)S(1)}, u32[]{:S(2)}, u32[]{:S(2)}) collective-permute-start(f32[2,8,1,128]{3,2,1,0:T(1,128)S(1)} %get-tuple-element.33), channel_id=1, source_target_pairs={{0,4},{4,8},{8,12},{12,16},{16,20},{20,24},{24,28},{28,0},{1,5},{5... | collective-permute-start | bytes 24584 | tf_op jit(solution)/shard_map/ppermute | solution.py:19
  123.6 4.9 %collective-permute-start.29 = (f32[2,8,1,128]{3,2,1,0:T(1,128)S(1)}, f32[2,8,1,128]{3,2,1,0:T(1,128)S(1)}, u32[]{:S(2)}, u32[]{:S(2)}) collective-permute-start(f32[2,8,1,128]{3,2,1,0:T(1,128)S(1)} %get-tuple-element.34), channel_id=1, source_target_pairs={{4,0},{8,4},{12,8},{16,12},{20,16},{24,20},{28,24},{0,28},{5,1},{9... | collective-permute-start | bytes 24584 | tf_op jit(solution)/shard_map/ppermute | solution.py:21
  128.8 10.6 %collective-permute-start.30 = (f32[2,8,34,1]{3,2,1,0:T(8,128)S(1)}, f32[2,8,34,1]{3,2,1,0:T(8,128)S(1)}, u32[]{:S(2)}, u32[]{:S(2)}) collective-permute-start(f32[2,8,34,1]{3,2,1,0:T(8,128)S(1)} %get-tuple-element.24), channel_id=1, source_target_pairs={{1,0},{2,1},{3,2},{0,3},{5,4},{6,5},{7,6},{4,7},{9,8},{10,9},{11,1... | collective-permute-start | bytes 6536 | tf_op jit(solution)/shard_map/ppermute | solution.py:21
  129.8 13.9 %collective-permute-start.31 = (f32[2,8,34,1]{3,2,1,0:T(8,128)S(1)}, f32[2,8,34,1]{3,2,1,0:T(8,128)S(1)}, u32[]{:S(2)}, u32[]{:S(2)}) collective-permute-start(f32[2,8,34,1]{3,2,1,0:T(8,128)S(1)} %get-tuple-element.23), channel_id=1, source_target_pairs={{0,1},{1,2},{2,3},{3,0},{4,5},{5,6},{6,7},{7,4},{8,9},{9,10},{10,1... | collective-permute-start | bytes 6536 | tf_op jit(solution)/shard_map/ppermute | solution.py:19
  160.2 9.2 %all-to-all-start.1 = ((bf16[4,8,1024]{2,0,1:T(4,128)(2,1)}), bf16[4,8,1024]{2,0,1:T(4,128)(2,1)S(1)}, u32[]{:S(2)}, u32[]{:S(2)}) async-start(bf16[4,8,1024]{2,0,1:T(4,128)(2,1)} %copy.32), calls=%async_computation.1 | async-start | bytes 131072 | tf_op jit(solution)/shard_map/all_to_all | solution.py:114
  170.1 14.8 %all-to-all-start.2 = ((bf16[4,8,1024]{2,1,0:T(8,128)(2,1)}), bf16[4,8,1024]{2,1,0:T(8,128)(2,1)S(1)}, u32[]{:S(2)}, u32[]{:S(2)}) async-start(bf16[4,8,1024]{2,1,0:T(8,128)(2,1)} %copy.33), calls=%async_computation.2 | async-start | bytes 131072 | tf_op jit(solution)/shard_map/all_to_all | solution.py:113
  206.2 8.8 %all-to-all-start.4 = ((bf16[4,8,1024]{2,1,0:T(8,128)(2,1)}), bf16[4,8,1024]{2,1,0:T(8,128)(2,1)S(1)}, u32[]{:S(2)}, u32[]{:S(2)}) async-start(bf16[4,8,1024]{2,1,0:T(8,128)(2,1)} %copy.37), calls=%async_computation.4 | async-start | bytes 131072 | tf_op jit(solution)/shard_map/all_to_all | solution.py:127
  234.0 7.1 %collective-permute-start.34 = (f32[1,8,34,1]{3,2,1,0:T(8,128)S(1)}, f32[1,8,34,1]{3,2,1,0:T(8,128)S(1)}, u32[]{:S(2)}, u32[]{:S(2)}) collective-permute-start(f32[1,8,34,1]{3,2,1,0:T(8,128)S(1)} %get-tuple-element.47), channel_id=1, source_target_pairs={{1,0},{2,1},{3,2},{0,3},{5,4},{6,5},{7,6},{4,7},{9,8},{10,9},{11,1... | collective-permute-start | bytes 3272 | tf_op jit(solution)/shard_map/ppermute | solution.py:21
  234.8 8.6 %collective-permute-start.35 = (f32[1,8,34,1]{3,2,1,0:T(8,128)S(1)}, f32[1,8,34,1]{3,2,1,0:T(8,128)S(1)}, u32[]{:S(2)}, u32[]{:S(2)}) collective-permute-start(f32[1,8,34,1]{3,2,1,0:T(8,128)S(1)} %get-tuple-element.48), channel_id=1, source_target_pairs={{0,1},{1,2},{2,3},{3,0},{4,5},{5,6},{6,7},{7,4},{8,9},{9,10},{10,1... | collective-permute-start | bytes 3272 | tf_op jit(solution)/shard_map/ppermute | solution.py:19
  243.6 4.9 %collective-permute-start.36 = (f32[2,8,1,128]{3,2,1,0:T(1,128)S(1)}, f32[2,8,1,128]{3,2,1,0:T(1,128)S(1)}, u32[]{:S(2)}, u32[]{:S(2)}) collective-permute-start(f32[2,8,1,128]{3,2,1,0:T(1,128)S(1)} %get-tuple-element.31), channel_id=1, source_target_pairs={{0,4},{4,8},{8,12},{12,16},{16,20},{20,24},{24,28},{28,0},{1,5},{5... | collective-permute-start | bytes 24584 | tf_op jit(solution)/shard_map/ppermute | solution.py:19
  248.8 10.6 %collective-permute-start.38 = (f32[2,8,34,1]{3,2,1,0:T(8,128)S(1)}, f32[2,8,34,1]{3,2,1,0:T(8,128)S(1)}, u32[]{:S(2)}, u32[]{:S(2)}) collective-permute-start(f32[2,8,34,1]{3,2,1,0:T(8,128)S(1)} %get-tuple-element.22), channel_id=1, source_target_pairs={{1,0},{2,1},{3,2},{0,3},{5,4},{6,5},{7,6},{4,7},{9,8},{10,9},{11,1... | collective-permute-start | bytes 6536 | tf_op jit(solution)/shard_map/ppermute | solution.py:21
  250.3 14.0 %collective-permute-start.39 = (f32[2,8,34,1]{3,2,1,0:T(8,128)S(1)}, f32[2,8,34,1]{3,2,1,0:T(8,128)S(1)}, u32[]{:S(2)}, u32[]{:S(2)}) collective-permute-start(f32[2,8,34,1]{3,2,1,0:T(8,128)S(1)} %get-tuple-element.21), channel_id=1, source_target_pairs={{0,1},{1,2},{2,3},{3,0},{4,5},{5,6},{6,7},{7,4},{8,9},{9,10},{10,1... | collective-permute-start | bytes 6536 | tf_op jit(solution)/shard_map/ppermute | solution.py:19
  (17 other events, 259.1 us)
